TPU v7x, 128 devices: a whole 4x4x4 slice. The times are simulated.
128 devices in a mesh: pts: 32 (over x, y, core), grp: 4 (over z).
Axes of the slice: x: 4, y: 4, z: 4, core: 2. Of those that a mesh axis runs over, the one named last changes fastest.
Arguments:
- points: bfloat16 [262144, 256], P(('pts', 'grp')), may hold values from -6 to 6
- cotangent: bfloat16 [262144, 256], P(('pts', 'grp')), may hold values from -24 to 24
- gain_one: float32 [256], replicated, may hold values from 0.25 to 1.75
- gain_two: float32 [256], replicated, may hold values from 0.25 to 1.75
- w_mid: bfloat16 [256, 256], replicated, may hold values from -0.375 to 0.375
- w_feat: bfloat16 [256, 256], replicated, may hold values from -0.375 to 0.375
- w_out: bfloat16 [256, 256], replicated, may hold values from -0.375 to 0.375
- w_up: bfloat16 [256, 1024], replicated, may hold values from -0.375 to 0.375
- w_down: bfloat16 [256, 1024], replicated, may hold values from -0.1875 to 0.1875
- w_slice: float32 [32, 32], replicated, as said below
- w_temp: float32 [32], replicated, may hold values from -2 to 2
- query_matrix: float32 [32, 32], replicated
- key_matrix: float32 [32, 32], replicated
- value_matrix: float32 [32, 32], replicated, may hold values from -1 to 1
Outputs:
- grad_points: bfloat16 [262144, 256], P(('pts', 'grp'))
- grad_mid: float32 [256, 256], replicated
- grad_feat: float32 [256, 256], replicated
- grad_out: float32 [256, 256], replicated
- grad_up: float32 [256, 1024], replicated
- grad_down: float32 [256, 1024], replicated
- grad_gain_one: float32 [256], replicated
- grad_gain_two: float32 [256], replicated
- grad_slice: float32 [32, 32], replicated
- grad_temp: float32 [32], replicated
- grad_query: float32 [32, 32], replicated
- grad_key: float32 [32, 32], replicated
- grad_value: float32 [32, 32], replicated
Inputs may be any that keep to these rules, and one draw needn't show every extreme that they name: w_slice is a real matrix.
All inputs are finite; a program needn't handle non-finite values.
Results may differ from a plain program's by a relative error of at most 0.023.
The roundings to bfloat16 on the way count: a program that leaves them out, or rounds other values in their place, can miss the bound.
Values sent between devices are 32-bit elements; how exact they have to be, the bound alone decides.
A program may use at most 128 MiB of HBM per device.

v0:
```python
import jax
import jax.numpy as jnp
from jax import lax
from jax.sharding import PartitionSpec as P

HEADS = 8
HEAD_DIM = 32
EPS_NORM = 1e-05
EPS_SLICE = 1e-05
PRECISION_LEVEL = lax.Precision.HIGHEST


def layer_norm(value_rows, gain):
    centred = value_rows - jnp.mean(value_rows, axis=-1, keepdims=True)
    spread_tokens = jnp.mean(centred * centred, axis=-1, keepdims=True)
    return centred * lax.rsqrt(spread_tokens + EPS_NORM) * gain


def assign(middle, w_slice, w_temp):
    temper = 0.5 + jax.nn.softplus(
        jnp.einsum("nhd,d->nh", middle, w_temp, precision=PRECISION_LEVEL)
    )
    logits = (
        jnp.einsum("nhd,dm->nhm", middle, w_slice, precision=PRECISION_LEVEL) / temper[:, :, None]
    )
    return jax.nn.softmax(logits, axis=-1)


def mix_tokens(numerator_sums, denom, query_matrix, key_matrix, value_matrix):
    slice_token_rows = numerator_sums / (denom[:, :, None] + EPS_SLICE)
    query_rows = jnp.einsum(
        "xsf,fz->xsz", slice_token_rows, query_matrix, precision=PRECISION_LEVEL
    )
    key_rows = jnp.einsum("xsf,fz->xsz", slice_token_rows, key_matrix, precision=PRECISION_LEVEL)
    value_rows = jnp.einsum(
        "xsf,fz->xsz", slice_token_rows, value_matrix, precision=PRECISION_LEVEL
    )
    scores = jnp.einsum(
        "hme,hne->hmn", query_rows, key_rows, precision=PRECISION_LEVEL
    ) * slice_token_rows.shape[-1] ** (-0.5)
    probs = jax.nn.softmax(scores, axis=-1)
    return jnp.einsum("hmn,hne->hme", probs, value_rows, precision=PRECISION_LEVEL)


def transposed(left, right):
    return lax.dot_general(
        left, right, (((0,), (0,)), ((), ())), preferred_element_type=jnp.float32
    )


def against(left, right):
    return lax.dot_general(
        left, right, (((1,), (1,)), ((), ())), preferred_element_type=jnp.float32
    )


def local(
    points,
    cotangent,
    gain_one,
    gain_two,
    w_mid,
    w_feat,
    w_out,
    w_up,
    w_down,
    w_slice,
    w_temp,
    query_matrix,
    key_matrix,
    value_matrix,
):
    rows = points.shape[0]
    width = w_mid.shape[0]
    hidden_units = w_up.shape[1]
    points_f = points.astype(jnp.float32)
    normed = layer_norm(points_f, gain_one).astype(jnp.bfloat16)
    middle = jnp.dot(normed, w_mid, preferred_element_type=jnp.float32).astype(jnp.bfloat16)
    feats = jnp.dot(normed, w_feat, preferred_element_type=jnp.float32).astype(jnp.bfloat16)
    middle_f = middle.astype(jnp.float32).reshape(rows, HEADS, HEAD_DIM)
    weights = assign(middle_f, w_slice, w_temp)
    weight_rows_low = weights.astype(jnp.bfloat16)
    feature_rows_three = feats.reshape(rows, HEADS, HEAD_DIM)
    numerator_sums = jnp.einsum(
        "gux,guj->uxj", weight_rows_low, feature_rows_three, preferred_element_type=jnp.float32
    )
    denom = jnp.sum(weights, axis=0)
    numerator_sums, denom = lax.psum((numerator_sums, denom), ("pts", "grp"))
    mixed_token_low = mix_tokens(
        numerator_sums, denom, query_matrix, key_matrix, value_matrix
    ).astype(jnp.bfloat16)
    spread_tokens = jnp.einsum(
        "lge,gex->lgx", weight_rows_low, mixed_token_low, preferred_element_type=jnp.float32
    )
    spread_tokens = spread_tokens.astype(jnp.bfloat16).reshape(rows, width)
    resid = (points_f + jnp.dot(spread_tokens, w_out, preferred_element_type=jnp.float32)).astype(
        jnp.bfloat16
    )
    resid_f = resid.astype(jnp.float32)
    normed_two = layer_norm(resid_f, gain_two).astype(jnp.bfloat16)
    pre = jnp.dot(normed_two, w_up, preferred_element_type=jnp.float32)
    hidden = jax.nn.gelu(pre).astype(jnp.bfloat16)
    d_hid = jnp.dot(cotangent, w_down, preferred_element_type=jnp.float32)
    gelu_back = jax.vjp(jax.nn.gelu, pre)[1]
    d_pre = gelu_back(d_hid)[0].astype(jnp.bfloat16)
    d_norm_two = against(d_pre, w_up)
    norm_back_two = jax.vjp(layer_norm, resid_f, gain_two)[1]
    d_res_ln, d_gain_two = norm_back_two(d_norm_two)
    d_resid = cotangent.astype(jnp.float32) + d_res_ln
    d_resid_b = d_resid.astype(jnp.bfloat16)
    spread_gradient = against(d_resid_b, w_out).astype(jnp.bfloat16).reshape(rows, HEADS, HEAD_DIM)
    mixed_gradient = jnp.einsum(
        "gux,guj->uxj", weight_rows_low, spread_gradient, preferred_element_type=jnp.float32
    )
    mixed_gradient = lax.psum(mixed_gradient, ("pts", "grp"))
    token_back = jax.vjp(mix_tokens, numerator_sums, denom, query_matrix, key_matrix, value_matrix)[
        1
    ]
    numerator_gradient, denominator_gradient, grad_query, grad_key, grad_value = token_back(
        mixed_gradient
    )
    weight_gradient = jnp.einsum(
        "wkt,klt->wkl", spread_gradient, mixed_token_low, preferred_element_type=jnp.float32
    )
    weight_gradient = (
        weight_gradient
        + jnp.einsum("wkt,klt->wkl", feature_rows_three.astype(jnp.float32), numerator_gradient)
        + denominator_gradient[None, :, :]
    )
    feature_gradient = jnp.einsum(
        "lge,gex->lgx", weight_rows_low.astype(jnp.float32), numerator_gradient
    )
    feature_gradient = feature_gradient.astype(jnp.bfloat16).reshape(rows, width)
    assign_back = jax.vjp(assign, middle_f, w_slice, w_temp)[1]
    d_mid, d_slice, d_temp = assign_back(weight_gradient)
    d_mid = d_mid.reshape(rows, width).astype(jnp.bfloat16)
    d_normed = against(d_mid, w_mid) + against(feature_gradient, w_feat)
    norm_back_one = jax.vjp(layer_norm, points_f, gain_one)[1]
    d_ln, d_gain_one = norm_back_one(d_normed)
    grad_points = (d_resid + d_ln).astype(jnp.bfloat16)

    def rows_of(left, right):
        return transposed(left, right)

    big = lax.psum(
        jnp.concatenate(
            [
                rows_of(normed, d_mid),
                rows_of(normed, feature_gradient),
                rows_of(spread_tokens, d_resid_b),
                rows_of(normed_two, d_pre),
                rows_of(cotangent, hidden),
            ],
            axis=1,
        ),
        ("pts", "grp"),
    )
    g_slice, g_temp, g_one, g_two = lax.psum(
        (d_slice, d_temp, d_gain_one, d_gain_two), ("pts", "grp")
    )
    return (
        grad_points,
        big[:, :width],
        big[:, width : 2 * width],
        big[:, 2 * width : 3 * width],
        big[:, 3 * width : 3 * width + hidden_units],
        big[:, 3 * width + hidden_units :],
        g_one,
        g_two,
        g_slice,
        g_temp,
        grad_query,
        grad_key,
        grad_value,
    )


def solution(mesh):
    return jax.shard_map(
        local,
        mesh=mesh,
        in_specs=(
            P(("pts", "grp"), None),
            P(("pts", "grp"), None),
            P(),
            P(),
            P(),
            P(),
            P(),
            P(),
            P(),
            P(),
            P(),
            P(),
            P(),
            P(),
        ),
        out_specs=(
            P(("pts", "grp"), None),
            P(),
            P(),
            P(),
            P(),
            P(),
            P(),
            P(),
            P(),
            P(),
            P(),
            P(),
            P(),
        ),
        check_vma=False,
    )
```

profile of v0, /device:TPU:1, one launch (start us, length us, event | category | flops | bytes accessed | tf_op | source)
XLA Modules:
  0.0 370.1 jit_solution(17323691424581522889)
XLA Ops:
  7.3 1.6 copy.28
  9.4 1.4 copy.27
  10.8 1.5 convolution_convert_fusion.3
  13.1 2.5 fusion.70
  15.5 6.6 %fusion.74 = f32[1,2048,8]{0,1,2:T(8,128)} fusion(bf16[2048,8,32]{0,2,1:T(8,128)(2,1)S(1)} %bitcast.132, f32[32]{0:T(128)S(1)} %copy-done.57), kind=kOutput, calls=%fused_computation.133 | convolution fusion | flops 6291456 | bytes 1114240 | tf_op jit(solution)/shard_map/nhd,d->nh/dot_general | solution.py:21
  22.1 5.2 %copy.46 = f32[1,2048,8]{1,2,0:T(8,128)S(1)} copy(f32[1,2048,8]{0,1,2:T(8,128)} %fusion.74) | data formatting | bytes 131072 | tf_op jit(solution)/shard_map/nhd,d->nh/dot_general | solution.py:21
  27.4 2.3 fusion.89
  30.1 1.6 copy-done.20
  32.2 70.0 %all-reduce.1 = (f32[8,32,32]{2,1,0:T(8,128)S(1)}, f32[8,32]{1,0:T(8,128)S(1)}) all-reduce(f32[8,32,32]{2,1,0:T(8,128)S(1)} %fusion.91, f32[8,32]{1,0:T(8,128)S(1)} %get-tuple-element.43), channel_id=1, replica_groups=mesh['pts'=32,'grp'=4] {'pts','grp'}, use_global_device_ids=true, to_apply=%region_4.5 | all-reduce | flops 8448 | bytes 67584 | tf_op jit(solution)/shard_map/psum | solution.py:88
  108.3 6.3 %fusion.7 = bf16[2048,1024]{1,0:T(8,128)(2,1)S(1)} fusion(f32[2048,1024]{1,0:T(8,128)S(1)} %fusion.43, bf16[2048,256]{1,0:T(8,128)(2,1)S(1)} %copy-done.27, bf16[256,1024]{1,0:T(8,128)(2,1)S(1)} %copy-done.59), kind=kOutput, calls=%fused_computation.9 | convolution fusion | flops 1115684864 | bytes 14155776 | tf_op jit(solution)/shard_map/dot_general | solution.py:103
  116.5 2.0 fusion.30
  121.8 63.1 %psum.58 = f32[8,32,32]{2,1,0:T(8,128)S(1)} all-reduce(f32[8,32,32]{2,1,0:T(8,128)S(1)} %fusion.93), channel_id=1, replica_groups=mesh['pts'=32,'grp'=4] {'pts','grp'}, use_global_device_ids=true, to_apply=%region_13.14 | all-reduce | flops 8192 | bytes 65536 | tf_op jit(solution)/shard_map/psum | solution.py:115
  194.8 2.1 fusion.22
  201.4 2.3 convolution_dynamic-update-slice_fusion
  203.8 4.3 %fusion.36 = f32[256,2816]{1,0:T(8,128)} fusion(f32[256,2816]{1,0:T(8,128)} %convolution_dynamic-update-slice_fusion, bf16[2048,256]{1,0:T(8,128)(2,1)S(1)} %copy-done.28, f32[2048,1024]{1,0:T(8,128)S(1)} %bitcast.126), kind=kOutput, calls=%fused_computation.60 | convolution fusion | flops 1092616192 | bytes 10485760 | tf_op jit(solution)/shard_map/dot_general | solution.py:46
  208.1 1.8 fusion.94
  210.7 1.5 fusion.28
  212.5 2.5 add_convert_fusion
  215.0 2.3 copy.44
  218.3 2.9 convolution_bitcast_fusion.3
  221.3 64.4 %all-reduce = (f32[256]{0:T(256)}, f32[256]{0:T(256)}, f32[32,32]{1,0:T(8,128)}, f32[32]{0:T(128)}) all-reduce(f32[256]{0:T(256)S(1)} %get-tuple-element.28, f32[256]{0:T(256)S(1)} %copy-done.56, f32[32,32]{1,0:T(8,128)S(1)} %convolution_bitcast_fusion.3, ...), channel_id=1, replica_groups=mesh['pts'=32,'grp'=4] {'pts','grp'}, use_global_device_ids=true, to_apply=%region_22.23 | all-reduce | flops 1568 | bytes 12544 | tf_op jit(solution)/shard_map/psum | solution.py:158
  288.9 69.1 %all-reduce.4.cloned.1.call-done = f32[256,2816]{1,0:T(8,128)} async-done(((f32[256,2816]{1,0:T(8,128)}), f32[256,2816]{1,0:T(8,128)}) %all-reduce.4.cloned.1.call-update) | async-done | bytes 2883600 | tf_op jit(solution)/shard_map/psum | solution.py:145
  358.0 2.0 fusion.88
  360.0 3.1 fusion.87
  (184 shorter events, 32.6 us)
Async XLA Ops:
  7.2 99.6 %copy-start = (bf16[256,1024]{1,0:T(8,128)(2,1)S(1)}, bf16[256,1024]{1,0:T(8,128)(2,1)}, u32[]{:S(2)}) copy-start(bf16[256,1024]{1,0:T(8,128)(2,1)} %param.21) | copy-start | bytes 1572868
  7.2 350.8 %all-reduce.4.cloned.1.call-start = ((), (), s32[]{:S(2)}) async-start(), calls=%async_computation | async-start | bytes 5767168 | tf_op jit(solution)/shard_map/psum | solution.py:145
  9.4 3.0 copy-start.30
  12.9 9.2 %copy-start.18 = (bf16[2048,256]{0,1:T(8,128)(2,1)}, bf16[2048,256]{0,1:T(8,128)(2,1)S(1)}, u32[]{:S(2)}) copy-start(bf16[2048,256]{0,1:T(8,128)(2,1)S(1)} %convolution_convert_fusion.4) | copy-start | bytes 3145732
  29.7 72.5 %copy-start.50 = (f32[32,32]{1,0:T(8,128)S(1)}, f32[32,32]{1,0:T(8,128)}, u32[]{:S(2)}) copy-start(f32[32,32]{1,0:T(8,128)} %param.26) | copy-start | bytes 12292
  30.1 75.2 %copy-start.1 = (bf16[2048,8,32]{0,2,1:T(8,128)(2,1)}, bf16[2048,8,32]{0,2,1:T(8,128)(2,1)S(1)}, u32[]{:S(2)}) copy-start(bf16[2048,8,32]{0,2,1:T(8,128)(2,1)S(1)} %get-tuple-element.44) | copy-start | bytes 3145732
  30.1 72.8 %copy-start.48 = (f32[32,32]{1,0:T(8,128)S(1)}, f32[32,32]{1,0:T(8,128)}, u32[]{:S(2)}) copy-start(f32[32,32]{1,0:T(8,128)} %param.27) | copy-start | bytes 12292
  30.1 73.1 %copy-start.52 = (f32[32,32]{1,0:T(8,128)S(1)}, f32[32,32]{1,0:T(8,128)}, u32[]{:S(2)}) copy-start(f32[32,32]{1,0:T(8,128)} %param.25) | copy-start | bytes 12292
  102.9 3.5 copy-start.33
  102.9 3.0 copy-start.29
  103.2 3.2 copy-start.42
  108.3 6.3 %copy-start.8 = (f32[2048,1024]{1,0:T(8,128)}, f32[2048,1024]{1,0:T(8,128)S(1)}, u32[]{:S(2)}) copy-start(f32[2048,1024]{1,0:T(8,128)S(1)} %fusion.43) | copy-start | bytes 25165828
  116.5 2.9 copy-start.4
  184.9 4.2 %copy-start.12 = (bf16[2048,256]{0,1:T(8,128)(2,1)S(1)}, bf16[2048,256]{0,1:T(8,128)(2,1)}, u32[]{:S(2)}) copy-start(bf16[2048,256]{0,1:T(8,128)(2,1)} %copy-done.11) | copy-start | bytes 3145732
  185.2 4.4 %copy-start.35 = (f32[8,32,32]{2,1,0:T(8,128)}, f32[8,32,32]{2,1,0:T(8,128)S(1)}, u32[]{:S(2)}) copy-start(f32[8,32,32]{2,1,0:T(8,128)S(1)} %fusion.56) | copy-start | bytes 98308
  186.5 3.1 copy-start.49
  191.6 6.7 %copy-start.22 = (bf16[8,32,2048]{2,1,0:T(8,128)(2,1)}, bf16[8,32,2048]{2,1,0:T(8,128)(2,1)S(1)}, u32[]{:S(2)}) copy-start(bf16[8,32,2048]{2,1,0:T(8,128)(2,1)S(1)} %convolution_convert_fusion.1) | copy-start | bytes 3145732
  194.7 6.7 %copy-start.61 = (bf16[2048,1024]{1,0:T(8,128)(2,1)S(1)}, bf16[2048,1024]{1,0:T(8,128)(2,1)}, u32[]{:S(2)}) copy-start(bf16[2048,1024]{1,0:T(8,128)(2,1)} %copy-done.60) | copy-start | bytes 12582916
  196.9 6.9 %slice-start = ((s8[8388608]{0:T(1024)(128)(4,1)}), s8[4194304]{0:T(1024)(128)(4,1)S(1)}, s32[]{:S(2)}) async-start(s8[8388608]{0:T(1024)(128)(4,1)} %bitcast.125), calls=%async_computation.1 | async-start | bytes 8388608
  200.2 3.6 slice-start.1
  218.3 2.9 copy-start.56
  218.3 67.3 %copy-start.39 = (f32[8,32,32]{2,1,0:T(8,128)S(1)}, f32[8,32,32]{2,1,0:T(8,128)}, u32[]{:S(2)}) copy-start(f32[8,32,32]{2,1,0:T(8,128)} %copy-done.37) | copy-start | bytes 98308
  218.3 68.4 %copy-start.41 = (f32[8,32,32]{2,1,0:T(8,128)S(1)}, f32[8,32,32]{2,1,0:T(8,128)}, u32[]{:S(2)}) copy-start(f32[8,32,32]{2,1,0:T(8,128)} %copy-done.40) | copy-start | bytes 98308
  218.3 69.5 %copy-start.36 = (f32[8,32,32]{2,1,0:T(8,128)S(1)}, f32[8,32,32]{2,1,0:T(8,128)}, u32[]{:S(2)}) copy-start(f32[8,32,32]{2,1,0:T(8,128)} %copy-done.35) | copy-start | bytes 98308
  (41 other events, 70.8 us)
Sparse Core Ops, SparseCore 0:
  208.2 149.6 all-reduce.3
where the time goes:
time: 376 us; the launch traced here: 370 us
  blocking collectives  197 us (52%)
  waiting for transfers between devices  69.1 us (18%)
  matrix products  54.2 us (14%)
  local copies, waits for them, and re-layouts  22.5 us (6%)
  between operations  15.2 us (4%)
  other arithmetic  11.5 us (3%)
    psum x1, blocking collectives, local(): numerator_sums, denom = lax.psum((numerator_sums, denom), ('pts', 'grp'))  70 us
    psum x1, waiting for transfers between devices, local(): lax.psum(jnp.concatenate([rows_of(normed, d_mid), rows_of(normed, feature...  69.1 us
    psum x1, blocking collectives, local(): lax.psum((d_slice, d_temp, d_gain_one, d_gain_two), ('pts', 'grp'))  64.4 us
    psum x1, blocking collectives, local(): mixed_gradient = lax.psum(mixed_gradient, ('pts', 'grp'))  63.1 us
    unnamed x131, local copies, waits for them, and re-layouts  12.2 us
    dot_general x5, matrix products, transposed(): lax.dot_general(left, right, (((0,), (0,)), ((), ())), preferred_element_...  10.6 us
  transfers between devices with their start and end apart: 1, of which 1 were waited for; matrix products, arithmetic and copies ran while one was open for 4% of the time, Pallas kernels for 0%

commit v1 on v0

--- a/solution.py
+++ b/solution.py
@@ -8,6 +8,11 @@
 EPS_NORM = 1e-05
 EPS_SLICE = 1e-05
 PRECISION_LEVEL = lax.Precision.HIGHEST
+
+
+def axis_by_axis(array, first, second):
+    partial = lax.psum(array, first)
+    return lax.psum(partial, second)
 
 
 def layer_norm(value_rows, gain):
@@ -155,8 +160,8 @@
         ),
         ("pts", "grp"),
     )
-    g_slice, g_temp, g_one, g_two = lax.psum(
-        (d_slice, d_temp, d_gain_one, d_gain_two), ("pts", "grp")
+    g_slice, g_temp, g_one, g_two = axis_by_axis(
+        (d_slice, d_temp, d_gain_one, d_gain_two), "grp", "pts"
     )
     return (
         grad_points,

time: 376 us -> 383 us (1.019)
  the two profiles are of different devices: /device:TPU:1 before, /device:TPU:0 now
where the time goes in v1:
time: 383 us; the launch traced here: 377 us
  blocking collectives  273 us (71%)
  matrix products  54.3 us (14%)
  local copies, waits for them, and re-layouts  22.5 us (6%)
  between operations  15.2 us (4%)
  other arithmetic  11.5 us (3%)
    psum x1, blocking collectives, axis_by_axis(): return lax.psum(partial, second)  124 us
    psum x1, blocking collectives, local(): numerator_sums, denom = lax.psum((numerator_sums, denom), ('pts', 'grp'))  69.5 us
    psum x1, blocking collectives, local(): mixed_gradient = lax.psum(mixed_gradient, ('pts', 'grp'))  62.8 us
    psum x1, blocking collectives, axis_by_axis(): partial = lax.psum(array, first)  16.8 us
    unnamed x129, local copies, waits for them, and re-layouts  12.2 us
    dot_general x5, matrix products, transposed(): lax.dot_general(left, right, (((0,), (0,)), ((), ())), preferred_element_...  10.7 us
  transfers between devices with their start and end apart: 1, of which 0 were waited for; matrix products, arithmetic and copies ran while one was open for 4% of the time, Pallas kernels for 0%

profile of v1, /device:TPU:0, one launch (start us, length us, event | category | flops | bytes accessed | tf_op | source)
XLA Modules:
  0.0 376.6 jit_solution(17413422152228989870)
XLA Ops:
  7.3 1.6 copy.28
  9.4 1.4 copy.27
  10.8 1.5 convolution_convert_fusion.3
  13.1 2.5 fusion.70
  15.5 6.5 %fusion.74 = f32[1,2048,8]{0,1,2:T(8,128)} fusion(bf16[2048,8,32]{0,2,1:T(8,128)(2,1)S(1)} %bitcast.132, f32[32]{0:T(128)S(1)} %copy-done.56), kind=kOutput, calls=%fused_computation.133 | convolution fusion | flops 6291456 | bytes 1114240 | tf_op jit(solution)/shard_map/nhd,d->nh/dot_general | solution.py:26
  22.1 5.2 %copy.46 = f32[1,2048,8]{1,2,0:T(8,128)S(1)} copy(f32[1,2048,8]{0,1,2:T(8,128)} %fusion.74) | data formatting | bytes 131072 | tf_op jit(solution)/shard_map/nhd,d->nh/dot_general | solution.py:26
  27.4 2.3 fusion.89
  30.1 1.6 copy-done.20
  32.2 69.5 %all-reduce = (f32[8,32,32]{2,1,0:T(8,128)S(1)}, f32[8,32]{1,0:T(8,128)S(1)}) all-reduce(f32[8,32,32]{2,1,0:T(8,128)S(1)} %fusion.91, f32[8,32]{1,0:T(8,128)S(1)} %get-tuple-element.47), channel_id=1, replica_groups=mesh['pts'=32,'grp'=4] {'pts','grp'}, use_global_device_ids=true, to_apply=%region_4.5 | all-reduce | flops 8448 | bytes 67584 | tf_op jit(solution)/shard_map/psum | solution.py:93
  107.8 6.3 %fusion.7 = bf16[2048,1024]{1,0:T(8,128)(2,1)S(1)} fusion(f32[2048,1024]{1,0:T(8,128)S(1)} %fusion.43, bf16[2048,256]{1,0:T(8,128)(2,1)S(1)} %copy-done.27, bf16[256,1024]{1,0:T(8,128)(2,1)S(1)} %copy-done.58), kind=kOutput, calls=%fused_computation.9 | convolution fusion | flops 1115684864 | bytes 14155776 | tf_op jit(solution)/shard_map/dot_general | solution.py:108
  116.0 2.0 fusion.30
  121.3 62.8 %psum.86 = f32[8,32,32]{2,1,0:T(8,128)S(1)} all-reduce(f32[8,32,32]{2,1,0:T(8,128)S(1)} %fusion.93), channel_id=1, replica_groups=mesh['pts'=32,'grp'=4] {'pts','grp'}, use_global_device_ids=true, to_apply=%region_13.14 | all-reduce | flops 8192 | bytes 65536 | tf_op jit(solution)/shard_map/psum | solution.py:120
  194.0 2.1 fusion.22
  200.7 2.3 convolution_dynamic-update-slice_fusion
  203.0 4.3 %fusion.36 = f32[256,2816]{1,0:T(8,128)} fusion(f32[256,2816]{1,0:T(8,128)} %convolution_dynamic-update-slice_fusion, bf16[2048,256]{1,0:T(8,128)(2,1)S(1)} %copy-done.28, f32[2048,1024]{1,0:T(8,128)S(1)} %bitcast.126), kind=kOutput, calls=%fused_computation.60 | convolution fusion | flops 1092616192 | bytes 10485760 | tf_op jit(solution)/shard_map/dot_general | solution.py:51
  207.4 1.8 fusion.94
  210.0 1.5 fusion.28
  211.8 2.5 add_convert_fusion
  214.3 2.3 copy.44
  217.6 2.9 convolution_bitcast_fusion.3
  220.6 16.8 %all-reduce.2 = (f32[256]{0:T(256)S(1)}, f32[256]{0:T(256)S(1)}, f32[32,32]{1,0:T(8,128)S(1)}, f32[32]{0:T(128)S(1)}) all-reduce(f32[256]{0:T(256)S(1)} %get-tuple-element.28, f32[256]{0:T(256)S(1)} %copy-done.55, f32[32,32]{1,0:T(8,128)S(1)} %convolution_bitcast_fusion.3, ...), channel_id=1, replica_groups=mesh['pts'=32,'grp'=4] {'grp'}, use_global_device_ids=true, to_apply=%region_22.23 | all-reduce | flops 1568 | bytes 12544 | tf_op jit(solution)/shard_map/psum | solution.py:14
  237.4 123.8 %all-reduce.1 = (f32[256]{0:T(256)}, f32[256]{0:T(256)}, f32[32,32]{1,0:T(8,128)}, f32[32]{0:T(128)}) all-reduce(f32[256]{0:T(256)S(1)} %get-tuple-element.36, f32[256]{0:T(256)S(1)} %get-tuple-element.37, f32[32,32]{1,0:T(8,128)S(1)} %get-tuple-element.38, f32[32]{0:T(128)S(1)} %get-tuple-element.39), channel_id=1, replica_groups=mesh['pts'=32,'grp'=4] {'pts'}, use_global_device_ids=true, to_apply=%region_23.24 | all-reduce | flops 1568 | bytes 12544 | tf_op jit(solution)/shard_map/psum | solution.py:15
  364.5 2.0 fusion.88
  366.5 3.1 fusion.87
  (183 shorter events, 32.6 us)
Async XLA Ops:
  7.2 99.1 %copy-start = (bf16[256,1024]{1,0:T(8,128)(2,1)S(1)}, bf16[256,1024]{1,0:T(8,128)(2,1)}, u32[]{:S(2)}) copy-start(bf16[256,1024]{1,0:T(8,128)(2,1)} %param.21) | copy-start | bytes 1572868
  7.2 357.3 %all-reduce.5.cloned.1.call-start = ((), (), s32[]{:S(2)}) async-start(), calls=%async_computation | async-start | bytes 5767168 | tf_op jit(solution)/shard_map/psum | solution.py:150
  9.4 3.0 copy-start.30
  12.9 2.6 copy-start.18
  29.7 72.0 %copy-start.49 = (f32[32,32]{1,0:T(8,128)S(1)}, f32[32,32]{1,0:T(8,128)}, u32[]{:S(2)}) copy-start(f32[32,32]{1,0:T(8,128)} %param.26) | copy-start | bytes 12292
  30.0 74.8 %copy-start.1 = (bf16[2048,8,32]{0,2,1:T(8,128)(2,1)}, bf16[2048,8,32]{0,2,1:T(8,128)(2,1)S(1)}, u32[]{:S(2)}) copy-start(bf16[2048,8,32]{0,2,1:T(8,128)(2,1)S(1)} %get-tuple-element.48) | copy-start | bytes 3145732
  30.1 72.3 %copy-start.47 = (f32[32,32]{1,0:T(8,128)S(1)}, f32[32,32]{1,0:T(8,128)}, u32[]{:S(2)}) copy-start(f32[32,32]{1,0:T(8,128)} %param.27) | copy-start | bytes 12292
  30.1 72.6 %copy-start.51 = (f32[32,32]{1,0:T(8,128)S(1)}, f32[32,32]{1,0:T(8,128)}, u32[]{:S(2)}) copy-start(f32[32,32]{1,0:T(8,128)} %param.25) | copy-start | bytes 12292
  102.3 3.5 copy-start.33
  102.3 2.9 copy-start.29
  102.7 3.2 copy-start.41
  107.7 6.3 %copy-start.8 = (f32[2048,1024]{1,0:T(8,128)}, f32[2048,1024]{1,0:T(8,128)S(1)}, u32[]{:S(2)}) copy-start(f32[2048,1024]{1,0:T(8,128)S(1)} %fusion.43) | copy-start | bytes 25165828
  116.0 2.9 copy-start.4
  184.2 4.2 %copy-start.12 = (bf16[2048,256]{0,1:T(8,128)(2,1)S(1)}, bf16[2048,256]{0,1:T(8,128)(2,1)}, u32[]{:S(2)}) copy-start(bf16[2048,256]{0,1:T(8,128)(2,1)} %copy-done.11) | copy-start | bytes 3145732
  184.5 4.4 %copy-start.35 = (f32[8,32,32]{2,1,0:T(8,128)}, f32[8,32,32]{2,1,0:T(8,128)S(1)}, u32[]{:S(2)}) copy-start(f32[8,32,32]{2,1,0:T(8,128)S(1)} %fusion.56) | copy-start | bytes 98308
  185.8 3.1 copy-start.48
  190.9 6.7 %copy-start.22 = (bf16[8,32,2048]{2,1,0:T(8,128)(2,1)}, bf16[8,32,2048]{2,1,0:T(8,128)(2,1)S(1)}, u32[]{:S(2)}) copy-start(bf16[8,32,2048]{2,1,0:T(8,128)(2,1)S(1)} %convolution_convert_fusion.1) | copy-start | bytes 3145732
  194.0 6.7 %copy-start.60 = (bf16[2048,1024]{1,0:T(8,128)(2,1)S(1)}, bf16[2048,1024]{1,0:T(8,128)(2,1)}, u32[]{:S(2)}) copy-start(bf16[2048,1024]{1,0:T(8,128)(2,1)} %copy-done.59) | copy-start | bytes 12582916
  196.1 2.8 copy-start.25
  196.2 6.9 %slice-start = ((s8[8388608]{0:T(1024)(128)(4,1)}), s8[4194304]{0:T(1024)(128)(4,1)S(1)}, s32[]{:S(2)}) async-start(s8[8388608]{0:T(1024)(128)(4,1)} %bitcast.125), calls=%async_computation.1 | async-start | bytes 8388608
  199.5 3.6 slice-start.1
  217.6 3.0 copy-start.55
  217.6 144.7 %copy-start.40 = (f32[8,32,32]{2,1,0:T(8,128)S(1)}, f32[8,32,32]{2,1,0:T(8,128)}, u32[]{:S(2)}) copy-start(f32[8,32,32]{2,1,0:T(8,128)} %copy-done.39) | copy-start | bytes 98308
  217.6 145.8 %copy-start.36 = (f32[8,32,32]{2,1,0:T(8,128)S(1)}, f32[8,32,32]{2,1,0:T(8,128)}, u32[]{:S(2)}) copy-start(f32[8,32,32]{2,1,0:T(8,128)} %copy-done.35) | copy-start | bytes 98308
  (40 other events, 68.0 us)
Sparse Core Ops, SparseCore 0:
  207.5 150.1 all-reduce.4
